TPU v7x, 128 devices: a whole 4x4x4 slice. The times are simulated.
128 devices in a mesh: rows: 16 (over z, x), sub: 8 (over y, core).
Axes of the slice: x: 4, y: 4, z: 4, core: 2. Of those that a mesh axis runs over, the one named last changes fastest.
Arguments:
- residuals: bfloat16 [65536, 1024], P(('rows', 'sub')), may hold values from -14 to 14
- codes: int32 [65536, 64], P(('rows', 'sub')), may hold values from 0 to 255, as said below
- codebook: bfloat16 [64, 16, 256], replicated, may hold values from -4 to 4
Outputs:
- rotated: bfloat16 [65536, 1024], P(('rows', 'sub'))
- new_codebook: float32 [64, 16, 256], P('sub', None, 'rows')
Inputs may be any that keep to these rules, and one draw needn't show every extreme that they name: `codes`: every codeword 0 to 255 occurs in every column.
All inputs are finite; a program needn't handle non-finite values.
Results may differ from a plain program's by a relative error of at most 0.0042.
Values may be sent and summed in bfloat16 or wider, within the bound.
A program may use at most 64 MiB of HBM per device.

v0:
```python
import jax
import jax.numpy as jnp
from jax import lax
from jax.sharding import PartitionSpec as P

D = 1024
SUBS = 64
CODES = 256
ITERS = 2


def rebuild(labels, codebook):
    rows = labels.shape[0]
    block = min(rows, 16384 // SUBS)
    levels = jnp.arange(CODES).astype(jnp.bfloat16)

    def one_block(piece):
        hot = (piece[:, :, None] == levels[None, None, :]).astype(jnp.bfloat16)
        rec = jnp.einsum("rmk,mdk->rmd", hot, codebook, preferred_element_type=jnp.float32)
        return rec.astype(jnp.bfloat16).reshape(block, D)

    return lax.map(one_block, labels.reshape(rows // block, block, SUBS)).reshape(rows, D)


def tally(values, labels, count):
    rows = values.shape[0]
    width = values.shape[1] // count
    block = min(rows, 16384 // count)
    levels = jnp.arange(CODES).astype(jnp.bfloat16)

    def one_step(index, carry):
        sums, totals = carry
        vals = lax.dynamic_slice_in_dim(values, index * block, block, 0).reshape(
            block, count, width
        )
        labs = lax.dynamic_slice_in_dim(labels, index * block, block, 0)
        hot = (labs[:, :, None] == levels[None, None, :]).astype(jnp.bfloat16)
        sums = sums + jnp.einsum("rmd,rmk->mdk", vals, hot, preferred_element_type=jnp.float32)
        totals = totals + jnp.sum(hot, axis=0, dtype=jnp.float32)
        return (sums, totals)

    start = (jnp.zeros((count, width, CODES), jnp.float32), jnp.zeros((count, CODES), jnp.float32))
    return lax.fori_loop(0, rows // block, one_step, start)


def iterate(polar, gram, make_gram):
    highest = lax.Precision.HIGHEST
    scale = jnp.sqrt(jnp.sqrt(jnp.sum(gram * gram) + 1e-06))
    polar = polar / scale
    gram = gram / (scale * scale)
    for step in range(ITERS):
        if step > 0:
            gram = make_gram(polar)
        moved = jnp.dot(polar, gram, precision=highest)
        polar = 3.4445 * polar - 4.775 * moved + 2.0315 * jnp.dot(moved, gram, precision=highest)
    return polar


def per_device(residuals, codes, codebook):
    labels = codes.astype(jnp.bfloat16)
    recon = rebuild(labels, codebook)
    highest = lax.Precision.HIGHEST
    contract = (((0,), (0,)), ((), ()))
    local = lax.dot_general(residuals, recon, contract, preferred_element_type=jnp.float32)
    cross = lax.psum(local, ("rows", "sub"))
    polar = cross / jnp.sqrt(jnp.sum(cross * cross) + 1e-06)

    def local_gram(current):
        return lax.dot_general(current, current, contract, precision=highest)

    polar = iterate(polar, local_gram(polar), local_gram)
    rotation = polar.astype(jnp.bfloat16)
    rotated = jnp.dot(residuals, rotation, preferred_element_type=jnp.float32).astype(jnp.bfloat16)
    owned_rows, owned_labels = (
        lax.all_to_all(rotated, "sub", split_axis=1, concat_axis=0, tiled=True),
        lax.all_to_all(labels, "sub", split_axis=1, concat_axis=0, tiled=True),
    )
    sums, totals = tally(owned_rows, owned_labels, owned_labels.shape[1])
    sums, totals = (
        lax.psum_scatter(sums, "rows", scatter_dimension=2, tiled=True),
        lax.psum_scatter(totals[:, None, :], "rows", scatter_dimension=2, tiled=True),
    )
    return (rotated, sums / totals)


def solution(mesh):
    return jax.shard_map(
        per_device,
        mesh=mesh,
        in_specs=(P(("rows", "sub"), None), P(("rows", "sub"), None), P()),
        out_specs=(P(("rows", "sub"), None), P("sub", None, "rows")),
        check_vma=False,
    )
```

profile of v0, /device:TPU:0, one launch (start us, length us, event | category | flops | bytes accessed | tf_op | source)
XLA Modules:
  0.0 439.1 jit_solution(3394257541561877917)
XLA Ops:
  8.2 8.8 %while.27 = (s32[]{:T(128)}, bf16[2,256,1024]{2,1,0:T(8,128)(2,1)S(1)}, bf16[2,256,64]{1,2,0:T(8,128)(2,1)S(1)}, bf16[64,16,256]{2,1,0:T(8,128)(2,1)}, s32[]{:T(128)}) while((s32[]{:T(128)}, bf16[2,256,1024]{2,1,0:T(8,128)(2,1)S(1)}, bf16[2,256,64]{1,2,0:T(8,128)(2,1)S(1)}, bf16[64,16,256]{2,1,0:T(8,128)(2,1)}, s32[]{:T(128)}) %tuple.70), condition=%wide.region_1.2_spmd.clone, body=%wide.region_0.1_spmd.clone.sunk | while | flops 138674432 | bytes 3245125 | solution.py:22
  8.3 4.1 fusion.45
  12.7 4.1 fusion.45
  17.1 3.3 convolution_bitcast_fusion
  20.3 156.7 %all-reduce.5.cloned.1.call-done = f32[1024,1024]{0,1:T(8,128)} async-done(((f32[1024,1024]{0,1:T(8,128)}), f32[1024,1024]{0,1:T(8,128)}) %all-reduce.5.cloned.1.call-update) | async-done | bytes 4194320 | tf_op jit(solution)/shard_map/psum | solution.py:65
  177.0 3.9 multiply_reduce_fusion.1
  181.6 19.1 %multiply_reduce_fusion = (f32[]{:T(128)}, f32[1024,1024]{1,0:T(8,128)}) fusion(f32[1024,1024]{0,1:T(8,128)} %all-reduce.5.cloned.1.call-done, f32[]{:T(128)S(6)} %sqrt.9), kind=kOutput, calls=%fused_computation.23 | convolution fusion | flops 12888047616 | bytes 8388616 | tf_op jit(solution)/shard_map/dot_general | solution.py:69
  201.4 18.0 %fusion.21 = f32[1024,1024]{1,0:T(8,128)} fusion(f32[1024,1024]{0,1:T(8,128)} %all-reduce.5.cloned.1.call-done, f32[]{:T(128)S(6)} %multiply.8, f32[1024,1024]{1,0:T(8,128)} %get-tuple-element.205, f32[]{:T(128)S(6)} %mul.38), kind=kOutput, calls=%fused_computation.31 | convolution fusion | flops 12886999040 | bytes 12582920 | tf_op jit(solution)/shard_map/dot_general | solution.py:54
  219.4 5.4 %copy.19 = f32[1024,1024]{0,1:T(8,128)} copy(f32[1024,1024]{1,0:T(8,128)} %fusion.21) | data formatting | bytes 8388608 | tf_op jit(solution)/shard_map/dot_general | solution.py:54
  224.7 27.6 %multiply_add_fusion = f32[1024,1024]{0,1:T(8,128)S(1)} fusion(f32[1024,1024]{0,1:T(8,128)} %copy.19, f32[1024,1024]{1,0:T(8,128)} %fusion.21, f32[1024,1024]{0,1:T(8,128)} %all-reduce.5.cloned.1.call-done, f32[]{:T(128)S(6)} %multiply.8, f32[1024,1024]{1,0:T(8,128)} %get-tuple-element.205, f32[]{:T(128)S(6)} %mul.38), kind=kOutput, calls=%fused_computation.22 | convolution fusion | flops 12892241920 | bytes 20971528 | tf_op jit(solution)/shard_map/dot_general | solution.py:55
  252.3 13.7 %fusion.22 = f32[1024,1024]{1,0:T(8,128)S(1)} fusion(f32[1024,1024]{0,1:T(8,128)S(1)} %multiply_add_fusion), kind=kOutput, calls=%fused_computation.36 | convolution fusion | flops 12884901888 | bytes 8388608 | tf_op jit(solution)/shard_map/dot_general | solution.py:69
  268.0 14.7 %fusion.23 = f32[1024,1024]{1,0:T(8,128)} fusion(f32[1024,1024]{0,1:T(8,128)S(1)} %multiply_add_fusion, f32[1024,1024]{1,0:T(8,128)S(1)} %fusion.22), kind=kOutput, calls=%fused_computation.37 | convolution fusion | flops 12884901888 | bytes 12582912 | tf_op jit(solution)/shard_map/dot_general | solution.py:54
  282.7 5.4 %copy.21 = f32[1024,1024]{0,1:T(8,128)} copy(f32[1024,1024]{1,0:T(8,128)} %fusion.23) | data formatting | bytes 8388608 | tf_op jit(solution)/shard_map/dot_general | solution.py:54
  288.1 19.3 %add_convert_fusion = bf16[1024,1024]{0,1:T(8,128)(2,1)S(1)} fusion(f32[1024,1024]{0,1:T(8,128)} %copy.21, f32[1024,1024]{0,1:T(8,128)} %copy-done.1, f32[1024,1024]{1,0:T(8,128)} %fusion.23, f32[1024,1024]{1,0:T(8,128)} %copy-done.2), kind=kOutput, calls=%fused_computation.21 | convolution fusion | flops 12891193344 | bytes 18874368 | tf_op jit(solution)/shard_map/dot_general | solution.py:55
  309.6 4.4 all-to-all-start
  314.6 15.3 %all-to-all-done = bf16[512,8,128]{0,2,1:T(8,128)(2,1)S(1)} async-done(((bf16[512,8,128]{0,2,1:T(8,128)(2,1)}), bf16[512,8,128]{0,2,1:T(8,128)(2,1)S(1)}, u32[]{:S(2)}, u32[]{:S(2)}) %all-to-all-start) | async-done | bytes 1048608 | tf_op jit(solution)/shard_map/all_to_all | solution.py:75
  330.0 3.4 all-to-all-start.1
  333.5 5.4 %all-to-all-done.1 = bf16[512,8,8]{0,2,1:T(8,128)(2,1)S(1)} async-done(((bf16[512,8,8]{0,2,1:T(8,128)(2,1)}), bf16[512,8,8]{0,2,1:T(8,128)(2,1)S(1)}, u32[]{:S(2)}, u32[]{:S(2)}) %all-to-all-start.1) | async-done | bytes 65568 | tf_op jit(solution)/shard_map/all_to_all | solution.py:76
  338.9 11.1 %while.28 = (s32[]{:T(128)}, f32[8,16,256]{2,1,0:T(8,128)S(1)}, f32[8,256]{1,0:T(8,128)S(1)}, bf16[4096,128]{0,1:T(8,128)(2,1)S(1)}, bf16[4096,8]{0,1:T(8,128)(2...) while((s32[]{:T(128)}, f32[8,16,256]{2,1,0:T(8,128)S(1)}, f32[8,256]{1,0:T(8,128)S(1)}, ...), condition=%wide.region_7.8_spmd.clone, body=%wide.region_5.7_spmd.clone.sunk | while | flops 155257088 | bytes 2000542 | solution.py:43
  338.9 2.9 fusion.48
  341.9 2.5 convert_reduce_fusion.2
  344.5 2.9 fusion.48
  354.2 39.1 %all-reduce.1 = f32[8,1,256]{2,0,1:T(8,128)S(1)} all-reduce(f32[8,1,256]{2,0,1:T(8,128)S(1)} %bitcast.64), channel_id=3, replica_groups=mesh['rows'=16,'sub'=8] {'rows'}, use_global_device_ids=true, to_apply=%region_9.10.clone | all-reduce | flops 2048 | bytes 16384
  393.4 36.8 %all-reduce.7.cloned.1.call-done = f32[8,16,256]{2,1,0:T(8,128)} async-done(((f32[8,16,256]{2,1,0:T(8,128)}), f32[8,16,256]{2,1,0:T(8,128)}) %all-reduce.7.cloned.1.call-update) | async-done | bytes 131088
  (45 shorter events, 14.4 us)
Async XLA Ops:
  7.2 9.9 %copy-start = (bf16[512,1024]{1,0:T(8,128)(2,1)S(1)}, bf16[512,1024]{1,0:T(8,128)(2,1)}, u32[]{:S(2)}) copy-start(bf16[512,1024]{1,0:T(8,128)(2,1)} %param.7) | copy-start | bytes 3145732
  7.2 169.9 %all-reduce.5.cloned.1.call-start = ((), (), s32[]{:S(2)}) async-start(), calls=%async_computation.2 | async-start | bytes 8388608 | tf_op jit(solution)/shard_map/psum | solution.py:65
  252.3 13.7 %copy-start.1 = (f32[1024,1024]{0,1:T(8,128)}, f32[1024,1024]{0,1:T(8,128)S(1)}, u32[]{:S(2)}) copy-start(f32[1024,1024]{0,1:T(8,128)S(1)} %multiply_add_fusion) | copy-start | bytes 12582916
  266.0 1.9 copy-start.2
  307.4 6.6 %copy-start.3 = (s32[512,64]{0,1:T(8,128)S(1)}, s32[512,64]{0,1:T(8,128)}, u32[]{:S(2)}) copy-start(s32[512,64]{0,1:T(8,128)} %param.8) | copy-start | bytes 393220
  309.6 20.3 %all-to-all-start = ((bf16[512,8,128]{0,2,1:T(8,128)(2,1)}), bf16[512,8,128]{0,2,1:T(8,128)(2,1)S(1)}, u32[]{:S(2)}, u32[]{:S(2)}) async-start(bf16[512,8,128]{0,2,1:T(8,128)(2,1)} %bitcast.3), calls=%async_computation | async-start | bytes 2097152 | tf_op jit(solution)/shard_map/all_to_all | solution.py:75
  330.0 8.9 %all-to-all-start.1 = ((bf16[512,8,8]{0,2,1:T(8,128)(2,1)}), bf16[512,8,8]{0,2,1:T(8,128)(2,1)S(1)}, u32[]{:S(2)}, u32[]{:S(2)}) async-start(bf16[512,8,8]{0,2,1:T(8,128)(2,1)} %convert_bitcast_fusion), calls=%async_computation.1 | async-start | bytes 131072 | tf_op jit(solution)/shard_map/all_to_all | solution.py:76
  333.3 97.0 %all-reduce.7.cloned.1.call-start = ((), (), s32[]{:S(2)}) async-start(), calls=%async_computation.3 | async-start | bytes 262144
  338.9 11.8 %copy-start.5 = (u32[128]{0:T(128)S(1)}, u32[128]{0:T(128)}, u32[]{:S(2)}) copy-start(u32[128]{0:T(128)} %constant.61) | copy-start | bytes 1540
  350.0 0.7 copy-start.4
Sparse Core Ops, SparseCore 0:
  20.5 156.5 all-reduce.4
  350.8 79.4 all-reduce.6
where the time goes:
time: 448 us; the launch traced here: 439 us
  waiting for transfers between devices  214 us (48%)
  matrix products  132 us (29%)
  blocking collectives  39.1 us (9%)
  local copies, waits for them, and re-layouts  17 us (4%)
  between operations  16.7 us (4%)
  other arithmetic  12.1 us (3%)
  starting transfers between devices  7.78 us (2%)
    psum x1, waiting for transfers between devices, per_device(): cross = lax.psum(local, ('rows', 'sub'))  157 us
    dot_general x2, matrix products, iterate(): jnp.dot(moved, gram, precision=highest)  46.9 us
    unnamed x1, blocking collectives  39.1 us
    unnamed x3, waiting for transfers between devices  36.9 us
    dot_general x2, matrix products, local_gram(): return lax.dot_general(current, current, contract, precision=highest)  32.8 us
    dot_general x2, matrix products, iterate(): moved = jnp.dot(polar, gram, precision=highest)  32.7 us
    all_to_all x1, waiting for transfers between devices, per_device(): lax.all_to_all(rotated, 'sub', split_axis=1, concat_axis=0, tiled=True)  15.3 us
    dot_general x2, local copies, waits for them, and re-layouts, iterate(): moved = jnp.dot(polar, gram, precision=highest)  10.7 us
  transfers between devices with their start and end apart: 4, of which 4 were waited for; matrix products, arithmetic and copies ran while one was open for 1% of the time, Pallas kernels for 0%

commit v1 on v0

v1 whole, which is shorter than its diff:
```python
import jax
import jax.numpy as jnp
from jax import lax
from jax.experimental import pallas as pl
from jax.experimental.pallas import tpu as pltpu
from jax.sharding import PartitionSpec as P

D = 1024
SUBS = 64
CODES = 256
SUBDIM = 16
LANES = 128
A, B, C = 3.4445, -4.775, 2.0315
MESH = pl.DeviceIdType.MESH
F32 = jnp.float32
BF16 = jnp.bfloat16
COLS = ((0, 384), (384, 384), (768, 256))
ORDERS = (("z", "x", "y"), ("x", "y", "z"), ("y", "z", "x"))
NT = (((1,), (1,)), ((), ()))


class Here:
    def __init__(self):
        rows, sub = lax.axis_index("rows"), lax.axis_index("sub")
        self.at = {"z": rows // 4, "x": rows % 4, "y": sub // 2, "c": sub % 2}

    def device(self, axis, value):
        at = dict(self.at)
        at[axis] = value
        return (at["z"] * 4 + at["x"], at["y"] * 2 + at["c"])

    def peers(self, axis):
        size = 2 if axis == "c" else 4
        me = self.at[axis]
        return [(j - 1, (me + j) % size) for j in range(1, size)]

    def greet(self):
        barrier = pltpu.get_barrier_semaphore()
        for axis in "czxy":
            for _, other in self.peers(axis):
                pl.semaphore_signal(
                    barrier, inc=1, device_id=self.device(axis, other), device_id_type=MESH
                )
        pl.semaphore_wait(barrier, 10)

    def send(self, src, dst, send_sem, recv_sem, axis, other):
        copy = pltpu.make_async_remote_copy(
            src_ref=src,
            dst_ref=dst,
            send_sem=send_sem,
            recv_sem=recv_sem,
            device_id=self.device(axis, other),
            device_id_type=MESH,
        )
        copy.start()
        return copy


def hot_of(labels_ref, m, levels):
    row = labels_ref[pl.ds(m, 1), :]
    return jnp.where(levels == row, 1.0, 0.0).astype(BF16)


def rows_of(start, size):
    return pl.ds(pl.multiple_of(start, size), size)


def cross_kernel(labels_ref, book_ref, x_ref, out_ref, recon, part, got0, got1, got2, got3, ssem, rsem):
    here = Here()
    rows = x_ref.shape[0]
    levels = lax.broadcasted_iota(jnp.int32, (CODES, rows), 0)

    def one(m, carry):
        hot = hot_of(labels_ref, m, levels)
        rec = jnp.dot(book_ref[m], hot, preferred_element_type=F32)
        recon[rows_of(m * SUBDIM, SUBDIM), :] = rec.astype(BF16)
        return carry

    lax.fori_loop(0, SUBS, one, 0, unroll=4)
    here.greet()
    core = here.at["c"]
    mine, theirs = rows_of(core * 512, 512), rows_of((1 - core) * 512, 512)
    pending = []
    flight = {}
    for t, (first, width) in enumerate(COLS):
        cols = pl.ds(first, width)
        part[:, cols] = jnp.dot(recon[...], x_ref[:, cols], preferred_element_type=F32)
        flight[t] = here.send(
            part.at[theirs, cols], got0.at[:, cols], ssem.at[t, 0, 0], rsem.at[t, 0, 0], "c", 1 - core
        )
    base = {}
    for t, (first, width) in enumerate(COLS):
        cols = pl.ds(first, width)
        flight[t].wait_recv()
        pending.append(flight[t])
        part[mine, cols] += got0[:, cols]
        base[t] = core * 512
    size = 512
    for k, got in enumerate((got1, got2, got3)):
        size = size // 4
        for t, (first, width) in enumerate(COLS):
            cols = pl.ds(first, width)
            axis = ORDERS[t][k]
            flight[t] = []
            for slot, other in here.peers(axis):
                flight[t].append(
                    here.send(
                        part.at[rows_of(base[t] + other * size, size), cols],
                        got.at[slot, :, cols],
                        ssem.at[t, k + 1, slot],
                        rsem.at[t, k + 1, slot],
                        axis,
                        other,
                    )
                )
        for t, (first, width) in enumerate(COLS):
            cols = pl.ds(first, width)
            base[t] = base[t] + here.at[ORDERS[t][k]] * size
            for copy in flight[t]:
                copy.wait_recv()
                pending.append(copy)
            block = rows_of(base[t], size)
            total = (part[block, cols] + got[0, :, cols]) + (got[1, :, cols] + got[2, :, cols])
            if k < 2:
                part[block, cols] = total
            else:
                out_ref[block, cols] = total
    for k in (2, 1, 0):
        for t, (first, width) in enumerate(COLS):
            cols = pl.ds(first, width)
            axis = ORDERS[t][k]
            flight[t] = []
            block = rows_of(base[t], size)
            for slot, other in here.peers(axis):
                flight[t].append(
                    here.send(
                        out_ref.at[block, cols],
                        out_ref.at[block, cols],
                        ssem.at[t, 4 + k, slot],
                        rsem.at[t, 4 + k, slot],
                        axis,
                        other,
                    )
                )
        for t in range(3):
            for copy in flight[t]:
                copy.wait_recv()
                pending.append(copy)
            base[t] = base[t] - here.at[ORDERS[t][k]] * size
        size = size * 4
    for t, (first, width) in enumerate(COLS):
        cols = pl.ds(first, width)
        flight[t] = here.send(
            out_ref.at[mine, cols], out_ref.at[mine, cols], ssem.at[t, 7, 0], rsem.at[t, 7, 0], "c", 1 - core
        )
    for t in range(3):
        flight[t].wait_recv()
        pending.append(flight[t])
    for copy in pending:
        copy.wait_send()


def reduced_cross(labels, codebook, residuals):
    rows = residuals.shape[0]
    vmem = pl.BlockSpec(memory_space=pltpu.VMEM)
    return pl.pallas_call(
        cross_kernel,
        out_shape=jax.ShapeDtypeStruct((D, D), F32),
        in_specs=[vmem] * 3,
        out_specs=vmem,
        scratch_shapes=[
            pltpu.VMEM((D, rows), BF16),
            pltpu.VMEM((D, D), F32),
            pltpu.VMEM((512, D), F32),
            pltpu.VMEM((3, 128, D), F32),
            pltpu.VMEM((3, 32, D), F32),
            pltpu.VMEM((3, 8, D), F32),
            pltpu.SemaphoreType.DMA((3, 8, 3)),
            pltpu.SemaphoreType.DMA((3, 8, 3)),
        ],
        compiler_params=pltpu.CompilerParams(
            collective_id=0, has_side_effects=True, vmem_limit_bytes=48 * 2**20
        ),
    )(labels, codebook, residuals)


def split(value):
    high = value.astype(BF16)
    return high, (value - high.astype(F32)).astype(BF16)


def dot3(ah, al, bh, bl, dims):
    def dot(a, b):
        return lax.dot_general(a, b, dims, preferred_element_type=F32)

    return dot(ah, bh) + (dot(ah, bl) + dot(al, bh))


STEP = 256


def symmetric(out, lh, ll, rh, rl):
    total = jnp.zeros((STEP, STEP), F32)
    for i in range(D // STEP):
        band = slice(i * STEP, (i + 1) * STEP)
        rest = slice(i * STEP, D)
        block = dot3(lh[band, :], ll[band, :], rh[rest, :], rl[rest, :], NT)
        out[band, rest] = block
        for j in range(i + 1, D // STEP):
            piece = block[:, (j - i) * STEP : (j - i + 1) * STEP]
            out[j * STEP : (j + 1) * STEP, band] = piece.T


def squares(ref):
    def one(i, total):
        block = ref[rows_of(i * 64, 64), :]
        return total + jnp.sum((block * block).reshape(8, 8, D), axis=0)

    total = lax.fori_loop(0, D // 64, one, jnp.zeros((8, D), F32))
    return jnp.sum(jnp.sum(total, axis=1, keepdims=True), axis=0, keepdims=True)


def iterate_kernel(cross_ref, labels_ref, x_ref, rot_ref, sums_ref, counts_ref, ah, al, gh, gl, gram, square):
    NN = (((1,), (0,)), ((), ()))
    norm = 1.0 / jnp.sqrt(squares(cross_ref) + 1e-06)

    def load(i, carry):
        band = rows_of(i * 64, 64)
        ah[band, :], al[band, :] = split(cross_ref[band, :] * norm)
        return carry

    lax.fori_loop(0, D // 64, load, 0)

    def split_gram(i, carry):
        band = rows_of(i * 64, 64)
        gh[band, :], gl[band, :] = split(gram[band, :])
        return carry

    for step in range(2):
        symmetric(gram, ah, al, ah, al)
        lax.fori_loop(0, D // 64, split_gram, 0)
        if step == 0:
            scale = jnp.sqrt(jnp.sqrt(squares(gram) + 1e-06))
            back = 1.0 / scale
        else:
            back = jnp.ones((1, 1), F32)
        ca, cb, cc = A * back, B * (back * back * back), C * (back * back * back * back * back)
        symmetric(square, gh, gl, gh, gl)

        def mix(i, carry):
            band = rows_of(i * 64, 64)
            row = lax.broadcasted_iota(jnp.int32, (64, D), 0) + i * 64
            col = lax.broadcasted_iota(jnp.int32, (64, D), 1)
            value = cb * gram[band, :] + cc * square[band, :]
            value = value + jnp.where(row == col, ca, 0.0)
            gh[band, :], gl[band, :] = split(value)
            return carry

        lax.fori_loop(0, D // 64, mix, 0)

        def move(i, carry):
            band = rows_of(i * STEP, STEP)
            square[band, :] = dot3(gh[band, :], gl[band, :], ah[...], al[...], NN)
            return carry

        lax.fori_loop(0, D // STEP, move, 0)

        def keep(i, carry):
            band = rows_of(i * 64, 64)
            ah[band, :], al[band, :] = split(square[band, :])
            return carry

        lax.fori_loop(0, D // 64, keep, 0)

    rows = x_ref.shape[0]
    rot_ref[...] = lax.dot_general(x_ref[...], ah[...], NT, preferred_element_type=F32).astype(BF16)
    levels = lax.broadcasted_iota(jnp.int32, (CODES, rows), 0)
    lane = lax.broadcasted_iota(jnp.int32, (CODES, LANES), 1)
    ones = jnp.ones((rows, LANES), BF16)
    counts_ref[...] = jnp.zeros_like(counts_ref)

    def tally(s, carry):
        cols = pl.ds(pl.multiple_of(s * LANES, LANES), LANES)
        side = jnp.concatenate([rot_ref[:, cols], ones], axis=1)
        sums = jnp.zeros((CODES, LANES), F32)
        counts = counts_ref[...]
        for mm in range(8):
            m = s * 8 + mm
            both = jnp.dot(hot_of(labels_ref, m, levels), side, preferred_element_type=F32)
            sums = jnp.where(lane // SUBDIM == mm, both[:, :LANES], sums)
            counts = jnp.where(lane == m, both[:, LANES:], counts)
        sums_ref[s] = sums
        counts_ref[...] = counts
        return carry

    lax.fori_loop(0, 8, tally, 0)


def rotate_and_tally(cross, labels, residuals):
    rows = residuals.shape[0]
    vmem = pl.BlockSpec(memory_space=pltpu.VMEM)
    return pl.pallas_call(
        iterate_kernel,
        out_shape=(
            jax.ShapeDtypeStruct((rows, D), BF16),
            jax.ShapeDtypeStruct((8, CODES, LANES), F32),
            jax.ShapeDtypeStruct((CODES, LANES), F32),
        ),
        in_specs=[vmem] * 3,
        out_specs=[vmem] * 3,
        scratch_shapes=[pltpu.VMEM((D, D), BF16)] * 4 + [pltpu.VMEM((D, D), F32)] * 2,
        compiler_params=pltpu.CompilerParams(vmem_limit_bytes=56 * 2**20),
    )(cross, labels, residuals)


def means_kernel(sums_ref, counts_ref, out_ref, half, g0, gc0, ga, gb, gc1, gc2, gd, ge, gf, ssem, rsem):
    here = Here()
    here.greet()
    z, x, y, core = (here.at[a] for a in "zxyc")
    pending = []
    number = [0]

    def go(src, dst, axis, other):
        n = number[0]
        number[0] += 1
        copy = here.send(src, dst, ssem.at[n], rsem.at[n], axis, other)
        pending.append(copy)
        return copy

    def got(copies):
        for copy in copies:
            copy.wait_recv()

    first = [go(sums_ref.at[:, 1 - core], g0, "c", 1 - core)]
    second = [go(counts_ref, gc0, "c", 1 - core)]
    got(first)
    for i in range(4):
        half[i] = sums_ref[i, core] + g0[i]
    za = [go(half.at[:, o, :, 0], ga.at[n], "z", o) for n, o in here.peers("z")]
    yb = [go(half.at[o, :, :, 1], gb.at[n], "y", o) for n, o in here.peers("y")]
    got(second)
    gc0[...] += counts_ref[...]
    zc = [go(gc0.at[o], gc1.at[n], "z", o) for n, o in here.peers("z")]
    got(za)
    half[:, z, :, 0] = half[:, z, :, 0] + ga[0] + ga[1] + ga[2]
    xa = [go(half.at[:, z, o, 0], gd.at[n], "x", o) for n, o in here.peers("x")]
    got(yb)
    half[y, :, :, 1] = half[y, :, :, 1] + gb[0] + gb[1] + gb[2]
    zb = [go(half.at[y, o, :, 1], ge.at[n], "z", o) for n, o in here.peers("z")]
    got(zc)
    gc0[z] = gc0[z] + gc1[0] + gc1[1] + gc1[2]
    xc = [go(gc0.at[z, o], gc2.at[n], "x", o) for n, o in here.peers("x")]
    got(xa)
    half[:, z, x, 0] = half[:, z, x, 0] + gd[0] + gd[1] + gd[2]
    ya = [go(half.at[o, z, x, 0], gf.at[0, n], "y", o) for n, o in here.peers("y")]
    got(zb)
    half[y, z, :, 1] = half[y, z, :, 1] + ge[0] + ge[1] + ge[2]
    xb = [go(half.at[y, z, o, 1], gf.at[1, n], "x", o) for n, o in here.peers("x")]
    got(xc)
    gc2[3] = gc0[z, x] + gc2[0] + gc2[1] + gc2[2]
    yc = [go(gc2.at[3], gc2.at[4 + n], "y", o) for n, o in here.peers("y")]
    got(ya)
    low = half[y, z, x, 0] + gf[0, 0] + gf[0, 1] + gf[0, 2]
    got(xb)
    high = half[y, z, x, 1] + gf[1, 0] + gf[1, 1] + gf[1, 2]
    got(yc)
    count = gc2[3] + gc2[4] + gc2[5] + gc2[6]
    row = lax.broadcasted_iota(jnp.int32, (LANES, LANES), 0)
    col = lax.broadcasted_iota(jnp.int32, (LANES, LANES), 1)
    spread = jnp.where(row == (y * 2 + core) * 8 + col // SUBDIM, 1.0, 0.0)
    count = jnp.dot(count, spread, precision=lax.Precision.HIGHEST, preferred_element_type=F32)
    mean = jnp.concatenate([low, high], axis=0) / count
    out_ref[...] = mean.T
    for copy in pending:
        copy.wait_send()


def means(sums, counts):
    vmem = pl.BlockSpec(memory_space=pltpu.VMEM)
    tile = (8, LANES)
    return pl.pallas_call(
        means_kernel,
        out_shape=jax.ShapeDtypeStruct((LANES, 16), F32),
        in_specs=[vmem] * 2,
        out_specs=vmem,
        scratch_shapes=[
            pltpu.VMEM((4, 4, 4, 2) + tile, F32),
            pltpu.VMEM((4, 4, 4, 2) + tile, F32),
            pltpu.VMEM((4, 4, 16, LANES), F32),
            pltpu.VMEM((3, 4, 4) + tile, F32),
            pltpu.VMEM((3, 4, 4) + tile, F32),
            pltpu.VMEM((3, 4, 16, LANES), F32),
            pltpu.VMEM((7, 16, LANES), F32),
            pltpu.VMEM((3, 4) + tile, F32),
            pltpu.VMEM((3, 4) + tile, F32),
            pltpu.VMEM((2, 3) + tile, F32),
            pltpu.SemaphoreType.DMA((32,)),
            pltpu.SemaphoreType.DMA((32,)),
        ],
        compiler_params=pltpu.CompilerParams(
            collective_id=1, has_side_effects=True, vmem_limit_bytes=32 * 2**20
        ),
    )(sums.reshape((4, 2, 4, 4, 2) + tile), counts.reshape(4, 4, 16, LANES))


def per_device(residuals, codes, codebook):
    labels = codes.T
    cross = reduced_cross(labels, codebook, residuals)
    rotated, sums, counts = rotate_and_tally(cross, labels, residuals)
    return rotated, means(sums, counts).reshape(8, SUBDIM, 16)


def solution(mesh):
    return jax.shard_map(
        per_device,
        mesh=mesh,
        in_specs=(P(("rows", "sub"), None), P(("rows", "sub"), None), P()),
        out_specs=(P(("rows", "sub"), None), P("sub", None, "rows")),
        check_vma=False,
    )
```

time: 448 us -> 135 us (0.30); the launches traced: 439 us -> 135 us
  waiting for transfers between devices: 214 us -> 0 us
  matrix products: 132 us -> 0 us
  Pallas kernels: 0 us -> 127 us
  blocking collectives: 39.1 us -> 0 us
  between operations: 16.7 us -> 0.67 us
  other arithmetic: 12.1 us -> 0 us
  local copies, waits for them, and re-layouts: 17 us -> 7.86 us
  starting transfers between devices: 7.78 us -> 0 us
    psum x1 -> x0, waiting for transfers between devices: 157 us -> none  [per_device(): cross = lax.psum(local, ('rows', 'sub'))]
    dot_general x12 -> x0, matrix products: 132 us -> none  [the longest x2 46.9 us: iterate(): jnp.dot(moved, gram, precision=highest)]
    pallas_call x0 -> x3, Pallas kernels: none -> 127 us  [the longest x1 57.9 us: reduced_cross(): pl.pallas_call(cross_kernel, out_shape=jax.ShapeDtypeStruct((D, D), F32),...]
    unnamed x1 -> x0, blocking collectives: 39.1 us -> none
    unnamed x3 -> x0, waiting for transfers between devices: 36.9 us -> none
    all_to_all x2 -> x0, waiting for transfers between devices: 20.7 us -> none  [the longest x1 15.3 us: per_device(): lax.all_to_all(rotated, 'sub', split_axis=1, concat_axis=0, tiled=True)]
    dot_general x2 -> x0, local copies, waits for them, and re-layouts: 10.7 us -> none  [iterate(): moved = jnp.dot(polar, gram, precision=highest)]
    reduce_sum x3 -> x0, other arithmetic: 8.92 us -> none  [the longest x2 5.05 us: one_step(): totals = totals + jnp.sum(hot, axis=0, dtype=jnp.float32)]
  transfers between devices with their start and end apart: 4 -> 0, of which waited for: 4 -> 0; matrix products, arithmetic and copies ran while one was open for 1% -> 0% of each run, Pallas kernels for 0% -> 0%
where the time goes in v1:
time: 135 us
  Pallas kernels  127 us (94%)
  local copies, waits for them, and re-layouts  7.86 us (6%)
    pallas_call x1, Pallas kernels, reduced_cross(): pl.pallas_call(cross_kernel, out_shape=jax.ShapeDtypeStruct((D, D), F32),...  57.9 us
    pallas_call x1, Pallas kernels, rotate_and_tally(): pl.pallas_call(iterate_kernel, out_shape=(jax.ShapeDtypeStruct((rows, D),...  50.1 us
    pallas_call x1, Pallas kernels, means(): pl.pallas_call(means_kernel, out_shape=jax.ShapeDtypeStruct((LANES, 16),...  18.6 us
    unnamed x13, local copies, waits for them, and re-layouts  7.86 us

profile of v1, /device:TPU:0, one launch (start us, length us, event | category | flops | bytes accessed | tf_op | source)
XLA Modules:
  0.0 135.2 jit_solution(3679145733132484562)
XLA Ops:
  0.6 0.0 copy-start.1
  0.6 1.2 copy-done.1
  1.9 0.0 copy-start.3
  1.9 1.0 copy-done.3
  2.9 0.0 copy-start.4
  2.9 0.9 copy-done.4
  3.8 57.9 %shard_map.50.cross_ref = f32[1024,1024]{1,0:T(8,128)S(1)} custom-call(s32[64,512]{1,0:T(8,128)S(1)} %bitcast.6, bf16[64,16,256]{2,1,0:T(8,128)(2,1)S(1)} %copy-done.3, bf16[512,1024]{1,0:T(8,128)(2,1)S(1)} %copy-done.1), custom_call_target="tpu_custom_call" | custom-call | tf_op jit(solution)/shard_map/pallas_call | solution.py:166
  61.7 0.0 copy-start
  61.7 1.9 %copy-done = f32[1024,1024]{1,0:T(8,128)} copy-done((f32[1024,1024]{1,0:T(8,128)}, f32[1024,1024]{1,0:T(8,128)S(1)}, u32[]{:S(2)}) %copy-start) | copy-done | bytes 4194328
  63.7 50.1 %shard_map.51 = (bf16[512,1024]{1,0:T(8,128)(2,1)}, f32[8,256,128]{2,1,0:T(8,128)}, f32[256,128]{1,0:T(8,128)}) custom-call(f32[1024,1024]{1,0:T(8,128)} %copy-done, s32[64,512]{1,0:T(8,128)} %bitcast.5, bf16[512,1024]{1,0:T(8,128)(2,1)} %x_ref.3), custom_call_target="tpu_custom_call" | custom-call | tf_op jit(solution)/shard_map/pallas_call | solution.py:302
  113.8 0.0 copy-start.2
  113.8 1.2 copy-done.2
  115.0 0.0 copy-start.5
  115.0 0.9 copy-done.5
  115.9 18.6 %shard_map.52 = f32[128,16]{1,0:T(8,128)S(1)} custom-call(f32[4,2,4,4,2,8,128]{6,5,4,3,2,1,0:T(8,128)S(1)} %bitcast.4, f32[4,4,16,128]{3,2,1,0:T(8,128)S(1)} %bitcast.8), custom_call_target="tpu_custom_call" | custom-call | tf_op jit(solution)/shard_map/pallas_call | solution.py:381
  134.6 0.6 copy.6
Async XLA Ops:
  0.6 1.2 copy-start.1
  1.9 1.0 copy-start.3
  2.9 0.9 copy-start.4
  61.7 1.9 %copy-start = (f32[1024,1024]{1,0:T(8,128)}, f32[1024,1024]{1,0:T(8,128)S(1)}, u32[]{:S(2)}) copy-start(f32[1024,1024]{1,0:T(8,128)S(1)} %shard_map.50.cross_ref) | copy-start | bytes 12582916
  113.8 1.2 copy-start.2
  115.0 0.9 copy-start.5

commit v2 on v0

v2 whole, which is shorter than its diff:
```python
import jax
import jax.numpy as jnp
from jax import lax
from jax.experimental import pallas as pl
from jax.experimental.pallas import tpu as pltpu
from jax.sharding import PartitionSpec as P

D = 1024
SUBS = 64
CODES = 256
SUBDIM = 16
LANES = 128
A, B, C = 3.4445, -4.775, 2.0315
MESH = pl.DeviceIdType.MESH
F32 = jnp.float32
BF16 = jnp.bfloat16
NN = (((1,), (0,)), ((), ()))
NT = (((1,), (1,)), ((), ()))
STEP = 256
BANDS = D // STEP
CHUNKS = (
    (0, 256, "z", "xy"),
    (256, 256, "x", "yz"),
    (512, 256, "y", "zx"),
    (768, 128, "z", "xy"),
    (896, 128, "x", "yz"),
)
EARLY, LATE = (0, 1, 2), (3, 4)
SPLIT = 768


class Here:
    def __init__(self, ssem, rsem):
        rows, sub = lax.axis_index("rows"), lax.axis_index("sub")
        self.at = {"z": rows // 4, "x": rows % 4, "y": sub // 2, "c": sub % 2}
        self.ssem, self.rsem, self.used = ssem, rsem, 0
        self.pending = []

    def device(self, **where):
        at = {**self.at, **where}
        return (at["z"] * 4 + at["x"], at["y"] * 2 + at["c"])

    def off(self, axis, by):
        return (self.at[axis] + by) % 4

    def send(self, src, dst, **where):
        copy = pltpu.make_async_remote_copy(
            src_ref=src,
            dst_ref=dst,
            send_sem=self.ssem.at[self.used],
            recv_sem=self.rsem.at[self.used],
            device_id=self.device(**where),
            device_id_type=MESH,
        )
        self.used += 1
        copy.start()
        self.pending.append(copy)
        return copy

    def greet(self):
        barrier = pltpu.get_barrier_semaphore()

        def signal(**where):
            pl.semaphore_signal(
                barrier, inc=1, device_id=self.device(**where), device_id_type=MESH
            )

        signal(c=1 - self.at["c"])
        for n in range(1, 64):
            signal(z=self.off("z", n // 16), x=self.off("x", n // 4 % 4), y=self.off("y", n % 4))

    def meet(self):
        pl.semaphore_wait(pltpu.get_barrier_semaphore(), 64)

    def drain(self):
        for copy in self.pending:
            copy.wait_send()
        self.pending = []


def arrive(copies):
    for copy in copies:
        copy.wait_recv()


def rows_of(start, size):
    return pl.ds(pl.multiple_of(start, size), size)


def dot(a, b, dims=NN):
    return lax.dot_general(a, b, dims, preferred_element_type=F32)


def split(value):
    high = value.astype(BF16)
    return high, (value - high.astype(F32)).astype(BF16)


def total_of(value):
    return jnp.sum(jnp.sum(value, axis=0, keepdims=True), axis=1, keepdims=True)


def diagonal():
    row = lax.broadcasted_iota(jnp.int32, (STEP, STEP), 0)
    return row == lax.broadcasted_iota(jnp.int32, (STEP, STEP), 1)


def upper(i, h, l, depth):
    band, rest = slice(i * STEP, (i + 1) * STEP), slice((i + 1) * STEP, D)
    mixed = dot(l[band, depth], h[band, depth], NT)
    block = dot(h[band, depth], h[band, depth], NT) + (mixed + mixed.T)
    if i == BANDS - 1:
        return block, None
    side = dot(h[band, depth], h[rest, depth], NT)
    side = side + (dot(h[band, depth], l[rest, depth], NT) + dot(l[band, depth], h[rest, depth], NT))
    return block, side


def store_split(h, l, i, block, side):
    band = slice(i * STEP, (i + 1) * STEP)
    h[band, band], l[band, band] = split(block)
    if side is not None:
        rest = slice((i + 1) * STEP, D)
        h[band, rest], l[band, rest] = split(side)
        h[rest, band], l[rest, band] = split(side.T)


def kernel(labels_hbm, book_hbm, x_hbm, rot_hbm, mean_ref, *scratch):
    (labels, book, x, hot, recon, part, full, got0, got1, got2, ah, al, gh, gl, qh, ql, bh, bl, rot) = scratch[:19]
    (slab, pair, sums_in, counts, countz, countx, county, local, ssem, rsem) = scratch[19:]
    here = Here(ssem, rsem)
    copies = [
        pltpu.make_async_copy(src, dst, local.at[n])
        for n, (src, dst) in enumerate(((labels_hbm, labels), (book_hbm, book), (x_hbm, x)))
    ]
    for copy in copies:
        copy.start()
    here.greet()
    z, xx, y, core = (here.at[a] for a in "zxyc")
    rows = x.shape[0]
    copies[0].wait()
    copies[1].wait()
    levels = lax.broadcasted_iota(jnp.int32, (CODES, rows), 0)

    def rebuild(m, carry):
        one = jnp.where(levels == labels[pl.ds(m, 1), :], 1.0, 0.0).astype(BF16)
        hot[m] = one
        recon[rows_of(m * SUBDIM, SUBDIM), :] = dot(book[m], one).astype(BF16)
        return carry

    lax.fori_loop(0, SUBS, rebuild, 0, unroll=8)
    copies[2].wait()
    here.meet()

    mine, theirs = rows_of(core * 512, 512), rows_of((1 - core) * 512, 512)
    flight, base = {}, {}

    def cols_of(t):
        return pl.ds(CHUNKS[t][0], CHUNKS[t][1])

    def stage_core(t):
        cols = cols_of(t)
        flight[t] = [here.send(part.at[theirs, cols], got0.at[:, cols], c=1 - core)]

    def stage_first(t):
        cols, axis = cols_of(t), CHUNKS[t][2]
        arrive(flight[t])
        part[mine, cols] += got0[:, cols]
        flight[t] = []
        for j in range(1, 4):
            other = here.off(axis, j)
            src = part.at[rows_of(core * 512 + other * 128, 128), cols]
            flight[t].append(here.send(src, got1.at[j - 1, :, cols], **{axis: other}))
        base[t] = core * 512 + here.at[axis] * 128

    def stage_second(t):
        cols, (p, q) = cols_of(t), CHUNKS[t][3]
        arrive(flight[t])
        block = rows_of(base[t], 128)
        part[block, cols] = (part[block, cols] + got1[0, :, cols]) + (got1[1, :, cols] + got1[2, :, cols])
        flight[t] = []
        for n in range(1, 16):
            i, j = here.off(p, n // 4), here.off(q, n % 4)
            src = part.at[rows_of(base[t] + (i * 4 + j) * 8, 8), cols]
            flight[t].append(here.send(src, got2.at[n - 1, :, cols], **{p: i, q: j}))

    def stage_back(t):
        cols, (p, q) = cols_of(t), CHUNKS[t][3]
        arrive(flight[t])
        own = rows_of(base[t] + (here.at[p] * 4 + here.at[q]) * 8, 8)
        total = part[own, cols]
        for n in range(15):
            total = total + got2[n, :, cols]
        full[own, cols] = total
        flight[t] = []
        for n in range(1, 16):
            i, j = here.off(p, n // 4), here.off(q, n % 4)
            flight[t].append(here.send(full.at[own, cols], full.at[own, cols], **{p: i, q: j}))

    def stage_wide(t):
        cols, axis = cols_of(t), CHUNKS[t][2]
        arrive(flight[t])
        block = rows_of(base[t], 128)
        flight[t] = []
        for j in range(1, 4):
            other = here.off(axis, j)
            flight[t].append(here.send(full.at[block, cols], full.at[block, cols], **{axis: other}))

    def stage_last(t):
        cols = cols_of(t)
        arrive(flight[t])
        flight[t] = [here.send(full.at[mine, cols], full.at[mine, cols], c=1 - core)]

    for first in range(0, D, STEP):
        cols = pl.ds(first, STEP)
        part[:, cols] = dot(recon[...], x[:, cols])
        for t in range(5):
            if first <= CHUNKS[t][0] < first + STEP:
                stage_core(t)
    for t in EARLY + LATE:
        stage_first(t)

    lane = lax.broadcasted_iota(jnp.int32, (CODES, LANES), 1)
    ones = jnp.ones((rows, LANES), BF16)
    counts[0] = jnp.zeros((CODES, LANES), F32)

    def count(g, carry):
        value = counts[0]
        for mm in range(8):
            m = g * 8 + mm
            value = jnp.where(lane == m, dot(hot[m], ones), value)
        counts[0] = value
        return carry

    lax.fori_loop(0, 8, count, 0)
    count_flight = [here.send(counts.at[0], counts.at[1], c=1 - core)]
    for t in EARLY:
        stage_second(t)
    arrive(count_flight)
    counts[2] = counts[0] + counts[1]
    count_flight = []
    for j in range(1, 4):
        other = here.off("z", j)
        src = counts.at[2, rows_of(other * 64, 64)]
        count_flight.append(here.send(src, countz.at[j - 1], z=other))
    for t in LATE:
        stage_second(t)
    for t in EARLY:
        stage_back(t)
    arrive(count_flight)
    countz[3] = (counts[2, rows_of(z * 64, 64)] + countz[0]) + (countz[1] + countz[2])
    count_flight = []
    for j in range(1, 4):
        other = here.off("x", j)
        count_flight.append(here.send(countz.at[3, rows_of(other * 16, 16)], countx.at[j - 1], x=other))
    for t in LATE:
        stage_back(t)
    for t in EARLY:
        stage_wide(t)
    arrive(count_flight)
    countx[3] = (countz[3, rows_of(xx * 16, 16)] + countx[0]) + (countx[1] + countx[2])
    count_flight = []
    for j in range(1, 4):
        count_flight.append(here.send(countx.at[3], county.at[j - 1], y=here.off("y", j)))
    for t in LATE:
        stage_wide(t)
    for t in EARLY:
        stage_last(t)
    for t in EARLY:
        arrive(flight[t])

    def load(cols):
        def one(i, carry):
            band = rows_of(i * 64, 64)
            ah[band, cols], al[band, cols] = split(full[band, cols])
            return carry

        lax.fori_loop(0, D // 64, one, 0)

    load(slice(0, SPLIT))
    here.drain()
    for t in LATE:
        stage_last(t)
    for i in range(BANDS):
        band, rest = slice(i * STEP, (i + 1) * STEP), slice((i + 1) * STEP, D)
        block, side = upper(i, ah, al, slice(0, SPLIT))
        part[band, band] = block
        if side is not None:
            part[band, rest] = side
    for t in LATE:
        arrive(flight[t])
    load(slice(SPLIT, D))
    trace, square = jnp.zeros((1, 1), F32), jnp.zeros((1, 1), F32)
    for i in range(BANDS):
        band, rest = slice(i * STEP, (i + 1) * STEP), slice((i + 1) * STEP, D)
        block, side = upper(i, ah, al, slice(SPLIT, D))
        block = block + part[band, band]
        trace += total_of(jnp.where(diagonal(), block, 0.0))
        square += total_of(block * block)
        part[band, band] = block
        if side is not None:
            side = side + part[band, rest]
            square += 2.0 * total_of(side * side)
            part[band, rest] = side
        store_split(gh, gl, i, block, side)

    norm = 1.0 / (trace + 1e-06)
    scale = jnp.sqrt(jnp.sqrt(square * norm * norm + 1e-06))
    unit = norm / (scale * scale)
    front = jnp.sqrt(norm) / scale

    def polynomial(front, unit):
        whole = slice(0, D)
        cb, cc = B * front * unit, C * front * unit
        for i in range(BANDS):
            band, rest = slice(i * STEP, (i + 1) * STEP), slice((i + 1) * STEP, D)
            block, side = upper(i, gh, gl, whole)
            block = cb * part[band, band] + cc * (unit * block)
            block = block + jnp.where(diagonal(), A * front, 0.0)
            if side is not None:
                side = cb * part[band, rest] + cc * (unit * side)
            store_split(qh, ql, i, block, side)

    def product(band, h, l):
        return dot(qh[band, :], h[...]) + (dot(qh[band, :], l[...]) + dot(ql[band, :], h[...]))

    polynomial(front, unit)

    def move(i, carry):
        band = rows_of(i * STEP, STEP)
        bh[band, :], bl[band, :] = split(product(band, ah, al))
        return carry

    lax.fori_loop(0, BANDS, move, 0)
    for i in range(BANDS):
        band, rest = slice(i * STEP, (i + 1) * STEP), slice((i + 1) * STEP, D)
        block, side = upper(i, bh, bl, slice(0, D))
        part[band, band] = block
        if side is not None:
            part[band, rest] = side
        store_split(gh, gl, i, block, side)
    one = jnp.ones((1, 1), F32)
    polynomial(one, one)

    outs = []
    for n in range(4):
        to = here.off("y", n + 1)
        band = rows_of(to * STEP, STEP)
        ah[band, :] = product(band, bh, bl).astype(BF16)
        rot[n] = dot(x[...], ah[band, :], NT).astype(BF16)
        outs.append(pltpu.make_async_copy(rot.at[n], rot_hbm.at[:, band], local.at[3 + n]))
        outs[n].start()
        for p in range(2):
            m = (to * 2 + p) * 8
            res = dot(hot[pl.ds(m, 8)].reshape(8 * CODES, rows), rot[n, :, p * LANES : (p + 1) * LANES])
            sums = res[:CODES]
            for mm in range(1, 8):
                sums = jnp.where(lane // SUBDIM == mm, res[mm * CODES : (mm + 1) * CODES], sums)
            slab[n, p] = sums
        swap = here.send(slab.at[n, 1 - core], pair.at[n], c=1 - core)
        swap.wait_recv()
        pair[n] += slab[n, core]
        for k in range(16):
            i, j = here.off("z", k // 4), here.off("x", k % 4)
            block = rows_of((i * 4 + j) * 16, 16)
            if n == 3 and k == 0:
                sums_in[n * 16 + k] = pair[n, block]
            else:
                flight[n, k] = here.send(pair.at[n, block], sums_in.at[n * 16 + k], z=i, x=j, y=to)
    arrive(count_flight)
    count = (countx[3] + county[0]) + (county[1] + county[2])
    row = lax.broadcasted_iota(jnp.int32, (LANES, LANES), 0)
    col = lax.broadcasted_iota(jnp.int32, (LANES, LANES), 1)
    spread = jnp.where(row == (y * 2 + core) * 8 + col // SUBDIM, 1.0, 0.0)
    count = jnp.dot(count, spread, precision=lax.Precision.HIGHEST, preferred_element_type=F32)
    sums = jnp.zeros((16, LANES), F32)
    for n in range(4):
        for k in range(16):
            if (n, k) != (3, 0):
                flight[n, k].wait_recv()
            sums = sums + sums_in[n * 16 + k]
    mean_ref[...] = (sums / count).T
    for copy in outs:
        copy.wait()
    here.drain()


def per_device(residuals, codes, codebook):
    rows = residuals.shape[0]
    anywhere = pl.BlockSpec(memory_space=pl.ANY)
    vmem = pltpu.VMEM
    matrix = [vmem((D, D), BF16)]
    rotated, mean = pl.pallas_call(
        kernel,
        out_shape=(
            jax.ShapeDtypeStruct((rows, D), BF16),
            jax.ShapeDtypeStruct((LANES, 16), F32),
        ),
        in_specs=[anywhere] * 3,
        out_specs=(anywhere, pl.BlockSpec(memory_space=pltpu.VMEM)),
        scratch_shapes=[
            vmem((SUBS, rows), jnp.int32),
            vmem((SUBS, SUBDIM, CODES), BF16),
            vmem((rows, D), BF16),
            vmem((SUBS, CODES, rows), BF16),
            vmem((D, rows), BF16),
            vmem((D, D), F32),
            vmem((D, D), F32),
            vmem((512, D), F32),
            vmem((3, 128, D), F32),
            vmem((15, 8, D), F32),
        ]
        + matrix * 8
        + [
            vmem((4, rows, STEP), BF16),
            vmem((4, 2, CODES, LANES), F32),
            vmem((4, CODES, LANES), F32),
            vmem((64, 16, LANES), F32),
            vmem((3, CODES, LANES), F32),
            vmem((4, 64, LANES), F32),
            vmem((4, 16, LANES), F32),
            vmem((3, 16, LANES), F32),
            pltpu.SemaphoreType.DMA((7,)),
            pltpu.SemaphoreType.DMA((272,)),
            pltpu.SemaphoreType.DMA((272,)),
        ],
        compiler_params=pltpu.CompilerParams(
            collective_id=0, has_side_effects=True, vmem_limit_bytes=62 * 2**20
        ),
    )(codes.T, codebook, residuals)
    return rotated, mean.reshape(8, SUBDIM, 16)


def solution(mesh):
    return jax.shard_map(
        per_device,
        mesh=mesh,
        in_specs=(P(("rows", "sub"), None), P(("rows", "sub"), None), P()),
        out_specs=(P(("rows", "sub"), None), P("sub", None, "rows")),
        check_vma=False,
    )
```

time: 448 us -> 104 us (0.23); the launches traced: 439 us -> 103 us
  waiting for transfers between devices: 214 us -> 0 us
  matrix products: 132 us -> 0 us
  Pallas kernels: 0 us -> 99.4 us
  blocking collectives: 39.1 us -> 0 us
  between operations: 16.7 us -> 0.65 us
  local copies, waits for them, and re-layouts: 17 us -> 2.93 us
  other arithmetic: 12.1 us -> 0 us
  starting transfers between devices: 7.78 us -> 0 us
    psum x1 -> x0, waiting for transfers between devices: 157 us -> none  [per_device(): cross = lax.psum(local, ('rows', 'sub'))]
    dot_general x12 -> x0, matrix products: 132 us -> none  [the longest x2 46.9 us: iterate(): jnp.dot(moved, gram, precision=highest)]
    pallas_call x0 -> x1, Pallas kernels: none -> 99.4 us  [per_device(): pl.pallas_call(kernel, out_shape=(jax.ShapeDtypeStruct((rows, D), BF16),...]
    unnamed x1 -> x0, blocking collectives: 39.1 us -> none
    unnamed x3 -> x0, waiting for transfers between devices: 36.9 us -> none
    all_to_all x2 -> x0, waiting for transfers between devices: 20.7 us -> none  [the longest x1 15.3 us: per_device(): lax.all_to_all(rotated, 'sub', split_axis=1, concat_axis=0, tiled=True)]
    dot_general x2 -> x0, local copies, waits for them, and re-layouts: 10.7 us -> none  [iterate(): moved = jnp.dot(polar, gram, precision=highest)]
    reduce_sum x3 -> x0, other arithmetic: 8.92 us -> none  [the longest x2 5.05 us: one_step(): totals = totals + jnp.sum(hot, axis=0, dtype=jnp.float32)]
  transfers between devices with their start and end apart: 4 -> 0, of which waited for: 4 -> 0; matrix products, arithmetic and copies ran while one was open for 1% -> 0% of each run, Pallas kernels for 0% -> 0%
where the time goes in v2:
time: 104 us; the launch traced here: 103 us
  Pallas kernels  99.4 us (96%)
  local copies, waits for them, and re-layouts  2.93 us (3%)
    pallas_call x1, Pallas kernels, per_device(): pl.pallas_call(kernel, out_shape=(jax.ShapeDtypeStruct((rows, D), BF16),...  99.4 us
    unnamed x4, local copies, waits for them, and re-layouts  2.93 us

profile of v2, /device:TPU:0, one launch (start us, length us, event | category | flops | bytes accessed | tf_op | source)
XLA Modules:
  0.0 103.0 jit_solution(16513309772944194149)
XLA Ops:
  0.6 99.4 %shard_map.50 = (bf16[512,1024]{1,0:T(8,128)(2,1)}, f32[128,16]{1,0:T(8,128)}) custom-call(s32[64,512]{1,0:T(8,128)} %bitcast.2, bf16[64,16,256]{2,1,0:T(8,128)(2,1)} %book_hbm.1, bf16[512,1024]{1,0:T(8,128)(2,1)} %x_hbm.1), custom_call_target="tpu_custom_call" | custom-call | tf_op jit(solution)/shard_map/pallas_call | solution.py:393
  100.0 0.0 copy-start
  100.1 2.3 %copy.7 = bf16[512,1024]{1,0:T(8,128)(2,1)} copy(bf16[512,1024]{1,0:T(8,128)(2,1)} %get-tuple-element.8) | data formatting | bytes 2097152
  102.4 0.0 copy-done
  102.4 0.6 copy.8
Async XLA Ops:
  100.0 2.3 %copy-start = (f32[128,16]{1,0:T(8,128)S(1)}, f32[128,16]{1,0:T(8,128)}, u32[]{:S(2)}) copy-start(f32[128,16]{1,0:T(8,128)} %get-tuple-element.5) | copy-start | bytes 24580

commit v3 on v2

--- a/solution.py
+++ b/solution.py
@@ -19,13 +19,16 @@
 STEP = 256
 BANDS = D // STEP
 CHUNKS = (
-    (0, 256, "z", "xy"),
-    (256, 256, "x", "yz"),
-    (512, 256, "y", "zx"),
+    (0, 128, "z", "xy"),
+    (128, 128, "x", "yz"),
+    (256, 128, "y", "zx"),
+    (384, 128, "z", "xy"),
+    (512, 128, "x", "yz"),
+    (640, 128, "y", "zx"),
     (768, 128, "z", "xy"),
     (896, 128, "x", "yz"),
 )
-EARLY, LATE = (0, 1, 2), (3, 4)
+GROUPS = ((0, 1, 2), (3, 4, 5), (6, 7))
 SPLIT = 768
 
 
@@ -66,16 +69,18 @@
             )
 
         signal(c=1 - self.at["c"])
-        for n in range(1, 64):
-            signal(z=self.off("z", n // 16), x=self.off("x", n // 4 % 4), y=self.off("y", n % 4))
+        for axis in "zxy":
+            for j in range(1, 4):
+                signal(**{axis: self.off(axis, j)})
 
     def meet(self):
-        pl.semaphore_wait(pltpu.get_barrier_semaphore(), 64)
-
-    def drain(self):
-        for copy in self.pending:
+        pl.semaphore_wait(pltpu.get_barrier_semaphore(), 10)
+
+    def drain(self, some=None):
+        done = list(self.pending) if some is None else some
+        for copy in done:
             copy.wait_send()
-        self.pending = []
+        self.pending = [copy for copy in self.pending if all(copy is not other for other in done)]
 
 
 def arrive(copies):
@@ -105,29 +110,39 @@
     return row == lax.broadcasted_iota(jnp.int32, (STEP, STEP), 1)
 
 
-def upper(i, h, l, depth):
-    band, rest = slice(i * STEP, (i + 1) * STEP), slice((i + 1) * STEP, D)
+def corner(i, h, l, depth=slice(0, D)):
+    band = slice(i * STEP, (i + 1) * STEP)
     mixed = dot(l[band, depth], h[band, depth], NT)
-    block = dot(h[band, depth], h[band, depth], NT) + (mixed + mixed.T)
-    if i == BANDS - 1:
-        return block, None
+    return dot(h[band, depth], h[band, depth], NT) + (mixed + mixed.T)
+
+
+def beside(i, rest, h, l, depth=slice(0, D)):
+    band = slice(i * STEP, (i + 1) * STEP)
     side = dot(h[band, depth], h[rest, depth], NT)
-    side = side + (dot(h[band, depth], l[rest, depth], NT) + dot(l[band, depth], h[rest, depth], NT))
-    return block, side
-
-
-def store_split(h, l, i, block, side):
-    band = slice(i * STEP, (i + 1) * STEP)
-    h[band, band], l[band, band] = split(block)
-    if side is not None:
-        rest = slice((i + 1) * STEP, D)
-        h[band, rest], l[band, rest] = split(side)
-        h[rest, band], l[rest, band] = split(side.T)
-
-
-def kernel(labels_hbm, book_hbm, x_hbm, rot_hbm, mean_ref, *scratch):
-    (labels, book, x, hot, recon, part, full, got0, got1, got2, ah, al, gh, gl, qh, ql, bh, bl, rot) = scratch[:19]
-    (slab, pair, sums_in, counts, countz, countx, county, local, ssem, rsem) = scratch[19:]
+    return side + (dot(h[band, depth], l[rest, depth], NT) + dot(l[band, depth], h[rest, depth], NT))
+
+
+def tiles(*bands):
+    for i in bands:
+        band, rest = slice(i * STEP, (i + 1) * STEP), slice((i + 1) * STEP, D)
+        yield i, band, band
+        if i < BANDS - 1:
+            yield i, band, rest
+
+
+def tile(i, band, cols, h, l, depth=slice(0, D)):
+    return corner(i, h, l, depth) if band == cols else beside(i, cols, h, l, depth)
+
+
+def store_split(h, l, band, cols, value):
+    h[band, cols], l[band, cols] = split(value)
+    if band != cols:
+        h[cols, band], l[cols, band] = split(value.T)
+
+
+def kernel(labels_hbm, book_hbm, x_hbm, rot_ref, mean_ref, *scratch):
+    (labels, book, x, hot, recon, part, full, got0, got1, got2, ah, al, gh, gl, qh, ql, bh, bl) = scratch[:18]
+    (slab, pair, sums_in, counts, countz, countx, county, local, ssem, rsem) = scratch[18:]
     here = Here(ssem, rsem)
     copies = [
         pltpu.make_async_copy(src, dst, local.at[n])
@@ -214,10 +229,10 @@
     for first in range(0, D, STEP):
         cols = pl.ds(first, STEP)
         part[:, cols] = dot(recon[...], x[:, cols])
-        for t in range(5):
+        for t in range(len(CHUNKS)):
             if first <= CHUNKS[t][0] < first + STEP:
                 stage_core(t)
-    for t in EARLY + LATE:
+    for t in range(len(CHUNKS)):
         stage_first(t)
 
     lane = lax.broadcasted_iota(jnp.int32, (CODES, LANES), 1)
@@ -234,8 +249,14 @@
 
     lax.fori_loop(0, 8, count, 0)
     count_flight = [here.send(counts.at[0], counts.at[1], c=1 - core)]
-    for t in EARLY:
-        stage_second(t)
+    def go(stage, g):
+        for t in GROUPS[g]:
+            stage(t)
+
+    for t in GROUPS[0]:
+        arrive(flight[t])
+        flight[t] = []
+    go(stage_second, 0)
     arrive(count_flight)
     counts[2] = counts[0] + counts[1]
     count_flight = []
@@ -243,66 +264,57 @@
         other = here.off("z", j)
         src = counts.at[2, rows_of(other * 64, 64)]
         count_flight.append(here.send(src, countz.at[j - 1], z=other))
-    for t in LATE:
-        stage_second(t)
-    for t in EARLY:
-        stage_back(t)
+    go(stage_second, 1)
+    go(stage_back, 0)
     arrive(count_flight)
     countz[3] = (counts[2, rows_of(z * 64, 64)] + countz[0]) + (countz[1] + countz[2])
     count_flight = []
     for j in range(1, 4):
         other = here.off("x", j)
         count_flight.append(here.send(countz.at[3, rows_of(other * 16, 16)], countx.at[j - 1], x=other))
-    for t in LATE:
-        stage_back(t)
-    for t in EARLY:
-        stage_wide(t)
+    go(stage_second, 2)
+    reads_part = list(here.pending)
+    go(stage_back, 1)
+    go(stage_wide, 0)
     arrive(count_flight)
     countx[3] = (countz[3, rows_of(xx * 16, 16)] + countx[0]) + (countx[1] + countx[2])
     count_flight = []
     for j in range(1, 4):
         count_flight.append(here.send(countx.at[3], county.at[j - 1], y=here.off("y", j)))
-    for t in LATE:
-        stage_wide(t)
-    for t in EARLY:
-        stage_last(t)
-    for t in EARLY:
+    go(stage_back, 2)
+    go(stage_wide, 1)
+    go(stage_wide, 2)
+    go(stage_last, 0)
+    go(stage_last, 1)
+    for t in GROUPS[0] + GROUPS[1]:
         arrive(flight[t])
 
     def load(cols):
         def one(i, carry):
             band = rows_of(i * 64, 64)
-            ah[band, cols], al[band, cols] = split(full[band, cols])
+            ah[band, cols], al[band, cols] = split(full[rows_of((i * 64 + core * 512) % D, 64), cols])
             return carry
 
         lax.fori_loop(0, D // 64, one, 0)
 
     load(slice(0, SPLIT))
-    here.drain()
-    for t in LATE:
-        stage_last(t)
-    for i in range(BANDS):
-        band, rest = slice(i * STEP, (i + 1) * STEP), slice((i + 1) * STEP, D)
-        block, side = upper(i, ah, al, slice(0, SPLIT))
-        part[band, band] = block
-        if side is not None:
-            part[band, rest] = side
-    for t in LATE:
+    here.drain(reads_part)
+    go(stage_last, 2)
+    for i, band, cols in tiles(0, 1, 2, 3):
+        part[band, cols] = tile(i, band, cols, ah, al, slice(0, SPLIT))
+    for t in GROUPS[2]:
         arrive(flight[t])
     load(slice(SPLIT, D))
     trace, square = jnp.zeros((1, 1), F32), jnp.zeros((1, 1), F32)
-    for i in range(BANDS):
-        band, rest = slice(i * STEP, (i + 1) * STEP), slice((i + 1) * STEP, D)
-        block, side = upper(i, ah, al, slice(SPLIT, D))
-        block = block + part[band, band]
-        trace += total_of(jnp.where(diagonal(), block, 0.0))
-        square += total_of(block * block)
-        part[band, band] = block
-        if side is not None:
-            side = side + part[band, rest]
-            square += 2.0 * total_of(side * side)
-            part[band, rest] = side
-        store_split(gh, gl, i, block, side)
+    for i, band, cols in tiles(0, 1, 2, 3):
+        value = tile(i, band, cols, ah, al, slice(SPLIT, D)) + part[band, cols]
+        if band == cols:
+            trace += total_of(jnp.where(diagonal(), value, 0.0))
+            square += total_of(value * value)
+        else:
+            square += 2.0 * total_of(value * value)
+        part[band, cols] = value
+        store_split(gh, gl, band, cols, value)
 
     norm = 1.0 / (trace + 1e-06)
     scale = jnp.sqrt(jnp.sqrt(square * norm * norm + 1e-06))
@@ -310,55 +322,76 @@
     front = jnp.sqrt(norm) / scale
 
     def polynomial(front, unit):
-        whole = slice(0, D)
         cb, cc = B * front * unit, C * front * unit
-        for i in range(BANDS):
-            band, rest = slice(i * STEP, (i + 1) * STEP), slice((i + 1) * STEP, D)
-            block, side = upper(i, gh, gl, whole)
-            block = cb * part[band, band] + cc * (unit * block)
-            block = block + jnp.where(diagonal(), A * front, 0.0)
-            if side is not None:
-                side = cb * part[band, rest] + cc * (unit * side)
-            store_split(qh, ql, i, block, side)
+        for i, band, cols in tiles(0, 1, 2, 3):
+            value = cb * part[band, cols] + cc * (unit * tile(i, band, cols, gh, gl))
+            if band == cols:
+                value = value + jnp.where(diagonal(), A * front, 0.0)
+            store_split(qh, ql, band, cols, value)
 
     def product(band, h, l):
         return dot(qh[band, :], h[...]) + (dot(qh[band, :], l[...]) + dot(ql[band, :], h[...]))
 
     polynomial(front, unit)
 
-    def move(i, carry):
-        band = rows_of(i * STEP, STEP)
+    halves = []
+    for i in range(2):
+        band, there = slice(i * STEP, (i + 1) * STEP), slice(512 + i * STEP, 512 + (i + 1) * STEP)
         bh[band, :], bl[band, :] = split(product(band, ah, al))
-        return carry
-
-    lax.fori_loop(0, BANDS, move, 0)
-    for i in range(BANDS):
-        band, rest = slice(i * STEP, (i + 1) * STEP), slice((i + 1) * STEP, D)
-        block, side = upper(i, bh, bl, slice(0, D))
-        part[band, band] = block
-        if side is not None:
-            part[band, rest] = side
-        store_split(gh, gl, i, block, side)
+        halves.append(here.send(bh.at[band], bh.at[there], c=1 - core))
+        halves.append(here.send(bl.at[band], bl.at[there], c=1 - core))
+
+    def gram(i, band, cols):
+        value = tile(i, band, cols, bh, bl)
+        part[band, cols] = value
+        store_split(gh, gl, band, cols, value)
+
+    low, high, right = slice(0, STEP), slice(STEP, 512), slice(512, D)
+    gram(0, low, low)
+    gram(0, low, high)
+    gram(1, high, high)
+    arrive(halves)
+    gram(0, low, right)
+    gram(1, high, right)
+    for i, band, cols in tiles(2, 3):
+        gram(i, band, cols)
     one = jnp.ones((1, 1), F32)
     polynomial(one, one)
 
-    outs = []
-    for n in range(4):
+    arrive(count_flight)
+    count = (countx[3] + county[0]) + (county[1] + county[2])
+    row = lax.broadcasted_iota(jnp.int32, (LANES, LANES), 0)
+    col = lax.broadcasted_iota(jnp.int32, (LANES, LANES), 1)
+    spread = jnp.where(row == (y * 2 + core) * 8 + col // SUBDIM, 1.0, 0.0)
+    count = jnp.dot(count, spread, precision=lax.Precision.HIGHEST, preferred_element_type=F32)
+
+    turned = {}
+
+    def turn(n):
         to = here.off("y", n + 1)
+        local = rows_of((to + 2 * core) % 4 * STEP + core * 128, 128)
+        band = rows_of(to * STEP + core * 128, 128)
+        ah[band, :] = product(local, bh, bl).astype(BF16)
+        turned[n] = [here.send(ah.at[band], ah.at[band], c=1 - core)]
+
+    def tally(n):
+        to = here.off("y", n + 1)
+        arrive(turned[n])
         band = rows_of(to * STEP, STEP)
-        ah[band, :] = product(band, bh, bl).astype(BF16)
-        rot[n] = dot(x[...], ah[band, :], NT).astype(BF16)
-        outs.append(pltpu.make_async_copy(rot.at[n], rot_hbm.at[:, band], local.at[3 + n]))
-        outs[n].start()
+        rot = dot(x[...], ah[band, :], NT).astype(BF16)
+        rot_ref[:, band] = rot
         for p in range(2):
             m = (to * 2 + p) * 8
-            res = dot(hot[pl.ds(m, 8)].reshape(8 * CODES, rows), rot[n, :, p * LANES : (p + 1) * LANES])
+            res = dot(hot[pl.ds(m, 8)].reshape(8 * CODES, rows), rot[:, p * LANES : (p + 1) * LANES])
             sums = res[:CODES]
             for mm in range(1, 8):
                 sums = jnp.where(lane // SUBDIM == mm, res[mm * CODES : (mm + 1) * CODES], sums)
             slab[n, p] = sums
-        swap = here.send(slab.at[n, 1 - core], pair.at[n], c=1 - core)
-        swap.wait_recv()
+        swap[n] = [here.send(slab.at[n, 1 - core], pair.at[n], c=1 - core)]
+
+    def spray(n):
+        to = here.off("y", n + 1)
+        arrive(swap[n])
         pair[n] += slab[n, core]
         for k in range(16):
             i, j = here.off("z", k // 4), here.off("x", k % 4)
@@ -366,22 +399,26 @@
             if n == 3 and k == 0:
                 sums_in[n * 16 + k] = pair[n, block]
             else:
-                flight[n, k] = here.send(pair.at[n, block], sums_in.at[n * 16 + k], z=i, x=j, y=to)
-    arrive(count_flight)
-    count = (countx[3] + county[0]) + (county[1] + county[2])
-    row = lax.broadcasted_iota(jnp.int32, (LANES, LANES), 0)
-    col = lax.broadcasted_iota(jnp.int32, (LANES, LANES), 1)
-    spread = jnp.where(row == (y * 2 + core) * 8 + col // SUBDIM, 1.0, 0.0)
-    count = jnp.dot(count, spread, precision=lax.Precision.HIGHEST, preferred_element_type=F32)
+                landed.append(here.send(pair.at[n, block], sums_in.at[n * 16 + k], z=i, x=j, y=to))
+
+    swap, landed = {}, []
+    turn(0)
+    turn(1)
+    tally(0)
+    turn(2)
+    tally(1)
+    spray(0)
+    turn(3)
+    tally(2)
+    spray(1)
+    tally(3)
+    spray(2)
+    spray(3)
     sums = jnp.zeros((16, LANES), F32)
-    for n in range(4):
-        for k in range(16):
-            if (n, k) != (3, 0):
-                flight[n, k].wait_recv()
-            sums = sums + sums_in[n * 16 + k]
+    arrive(landed)
+    for n in range(64):
+        sums = sums + sums_in[n]
     mean_ref[...] = (sums / count).T
-    for copy in outs:
-        copy.wait()
     here.drain()
 
 
@@ -397,7 +434,7 @@
             jax.ShapeDtypeStruct((LANES, 16), F32),
         ),
         in_specs=[anywhere] * 3,
-        out_specs=(anywhere, pl.BlockSpec(memory_space=pltpu.VMEM)),
+        out_specs=[pl.BlockSpec(memory_space=pltpu.VMEM)] * 2,
         scratch_shapes=[
             vmem((SUBS, rows), jnp.int32),
             vmem((SUBS, SUBDIM, CODES), BF16),
@@ -412,7 +449,6 @@
         ]
         + matrix * 8
         + [
-            vmem((4, rows, STEP), BF16),
             vmem((4, 2, CODES, LANES), F32),
             vmem((4, CODES, LANES), F32),
             vmem((64, 16, LANES), F32),
@@ -420,12 +456,12 @@
             vmem((4, 64, LANES), F32),
             vmem((4, 16, LANES), F32),
             vmem((3, 16, LANES), F32),
-            pltpu.SemaphoreType.DMA((7,)),
-            pltpu.SemaphoreType.DMA((272,)),
-            pltpu.SemaphoreType.DMA((272,)),
+            pltpu.SemaphoreType.DMA((3,)),
+            pltpu.SemaphoreType.DMA((400,)),
+            pltpu.SemaphoreType.DMA((400,)),
         ],
         compiler_params=pltpu.CompilerParams(
-            collective_id=0, has_side_effects=True, vmem_limit_bytes=62 * 2**20
+            collective_id=0, has_side_effects=True, vmem_limit_bytes=58 * 2**20
         ),
     )(codes.T, codebook, residuals)
     return rotated, mean.reshape(8, SUBDIM, 16)

time: 104 us -> 99.4 us (0.956)
  Pallas kernels: 99.4 us -> 94.7 us
    pallas_call x1, Pallas kernels: 99.4 us -> 94.7 us  [per_device(): pl.pallas_call(kernel, out_shape=(jax.ShapeDtypeStruct((rows, D), BF16),...]
where the time goes in v3:
time: 99.4 us; the launch traced here: 98.3 us
  Pallas kernels  94.7 us (95%)
  local copies, waits for them, and re-layouts  2.93 us (3%)
    pallas_call x1, Pallas kernels, per_device(): pl.pallas_call(kernel, out_shape=(jax.ShapeDtypeStruct((rows, D), BF16),...  94.7 us
    unnamed x4, local copies, waits for them, and re-layouts  2.93 us

profile of v3, /device:TPU:0, one launch (start us, length us, event | category | flops | bytes accessed | tf_op | source)
XLA Modules:
  0.0 98.3 jit_solution(1534288666105097817)
XLA Ops:
  0.6 94.7 %shard_map.50 = (bf16[512,1024]{1,0:T(8,128)(2,1)}, f32[128,16]{1,0:T(8,128)}) custom-call(s32[64,512]{1,0:T(8,128)} %bitcast.2, bf16[64,16,256]{2,1,0:T(8,128)(2,1)} %book_hbm.1, bf16[512,1024]{1,0:T(8,128)(2,1)} %x_hbm.1), custom_call_target="tpu_custom_call" | custom-call | tf_op jit(solution)/shard_map/pallas_call | solution.py:430
  95.3 0.0 copy-start
  95.4 2.3 %copy.7 = bf16[512,1024]{1,0:T(8,128)(2,1)} copy(bf16[512,1024]{1,0:T(8,128)(2,1)} %get-tuple-element.8) | data formatting | bytes 2097152
  97.6 0.0 copy-done
  97.6 0.6 copy.8
Async XLA Ops:
  95.3 2.3 %copy-start = (f32[128,16]{1,0:T(8,128)S(1)}, f32[128,16]{1,0:T(8,128)}, u32[]{:S(2)}) copy-start(f32[128,16]{1,0:T(8,128)} %get-tuple-element.5) | copy-start | bytes 24580

commit v4 on v3

--- a/solution.py
+++ b/solution.py
@@ -247,8 +247,7 @@
         counts[0] = value
         return carry
 
-    lax.fori_loop(0, 8, count, 0)
-    count_flight = [here.send(counts.at[0], counts.at[1], c=1 - core)]
+    lax.fori_loop(0, 3, count, 0)
     def go(stage, g):
         for t in GROUPS[g]:
             stage(t)
@@ -257,6 +256,13 @@
         arrive(flight[t])
         flight[t] = []
     go(stage_second, 0)
+    lax.fori_loop(3, 7, count, 0)
+    go(stage_second, 1)
+    lax.fori_loop(7, 8, count, 0)
+    count_flight = [here.send(counts.at[0], counts.at[1], c=1 - core)]
+    go(stage_back, 0)
+    go(stage_second, 2)
+    reads_part = list(here.pending)
     arrive(count_flight)
     counts[2] = counts[0] + counts[1]
     count_flight = []
@@ -264,28 +270,24 @@
         other = here.off("z", j)
         src = counts.at[2, rows_of(other * 64, 64)]
         count_flight.append(here.send(src, countz.at[j - 1], z=other))
-    go(stage_second, 1)
-    go(stage_back, 0)
+    go(stage_back, 1)
+    go(stage_wide, 0)
+    go(stage_back, 2)
     arrive(count_flight)
     countz[3] = (counts[2, rows_of(z * 64, 64)] + countz[0]) + (countz[1] + countz[2])
     count_flight = []
     for j in range(1, 4):
         other = here.off("x", j)
         count_flight.append(here.send(countz.at[3, rows_of(other * 16, 16)], countx.at[j - 1], x=other))
-    go(stage_second, 2)
-    reads_part = list(here.pending)
-    go(stage_back, 1)
-    go(stage_wide, 0)
+    go(stage_wide, 1)
+    go(stage_wide, 2)
+    go(stage_last, 0)
+    go(stage_last, 1)
     arrive(count_flight)
     countx[3] = (countz[3, rows_of(xx * 16, 16)] + countx[0]) + (countx[1] + countx[2])
     count_flight = []
     for j in range(1, 4):
         count_flight.append(here.send(countx.at[3], county.at[j - 1], y=here.off("y", j)))
-    go(stage_back, 2)
-    go(stage_wide, 1)
-    go(stage_wide, 2)
-    go(stage_last, 0)
-    go(stage_last, 1)
     for t in GROUPS[0] + GROUPS[1]:
         arrive(flight[t])
 
@@ -367,16 +369,17 @@
 
     turned = {}
 
-    def turn(n):
-        to = here.off("y", n + 1)
-        local = rows_of((to + 2 * core) % 4 * STEP + core * 128, 128)
-        band = rows_of(to * STEP + core * 128, 128)
+    def turn(pair_of_bands):
+        to = here.off("y", 2 * pair_of_bands + core + 1)
+        local = rows_of((to + 2 * core) % 4 * STEP, STEP)
+        band = rows_of(to * STEP, STEP)
         ah[band, :] = product(local, bh, bl).astype(BF16)
-        turned[n] = [here.send(ah.at[band], ah.at[band], c=1 - core)]
+        turned[pair_of_bands] = [here.send(ah.at[band], ah.at[band], c=1 - core)]
 
     def tally(n):
         to = here.off("y", n + 1)
-        arrive(turned[n])
+        if n % 2 == 0:
+            arrive(turned[n // 2])
         band = rows_of(to * STEP, STEP)
         rot = dot(x[...], ah[band, :], NT).astype(BF16)
         rot_ref[:, band] = rot
@@ -405,10 +408,8 @@
     turn(0)
     turn(1)
     tally(0)
-    turn(2)
     tally(1)
     spray(0)
-    turn(3)
     tally(2)
     spray(1)
     tally(3)
@@ -424,7 +425,7 @@
 
 def per_device(residuals, codes, codebook):
     rows = residuals.shape[0]
-    anywhere = pl.BlockSpec(memory_space=pl.ANY)
+    anywhere = pl.BlockSpec(memory_space=pltpu.HBM)
     vmem = pltpu.VMEM
     matrix = [vmem((D, D), BF16)]
     rotated, mean = pl.pallas_call(
@@ -461,7 +462,7 @@
             pltpu.SemaphoreType.DMA((400,)),
         ],
         compiler_params=pltpu.CompilerParams(
-            collective_id=0, has_side_effects=True, vmem_limit_bytes=58 * 2**20
+            collective_id=0, has_side_effects=True, vmem_limit_bytes=52 * 2**20
         ),
     )(codes.T, codebook, residuals)
     return rotated, mean.reshape(8, SUBDIM, 16)

time: 99.4 us -> 95.1 us (0.957)
  Pallas kernels: 94.7 us -> 89.8 us
    pallas_call x1, Pallas kernels: 94.7 us -> 89.8 us  [per_device(): pl.pallas_call(kernel, out_shape=(jax.ShapeDtypeStruct((rows, D), BF16),...]
    unnamed x4 -> x6, local copies, waits for them, and re-layouts: 2.93 us -> 3.54 us
where the time goes in v4:
time: 95.1 us; the launch traced here: 94 us
  Pallas kernels  89.8 us (94%)
  local copies, waits for them, and re-layouts  3.54 us (4%)
    pallas_call x1, Pallas kernels, per_device(): pl.pallas_call(kernel, out_shape=(jax.ShapeDtypeStruct((rows, D), BF16),...  89.8 us
    unnamed x6, local copies, waits for them, and re-layouts  3.54 us

profile of v4, /device:TPU:0, one launch (start us, length us, event | category | flops | bytes accessed | tf_op | source)
XLA Modules:
  0.0 94.0 jit_solution(17647867027196924617)
XLA Ops:
  0.6 0.0 copy-start
  0.6 1.0 %copy-done = bf16[64,16,256]{2,1,0:T(8,128)(2,1)S(1)} copy-done((bf16[64,16,256]{2,1,0:T(8,128)(2,1)S(1)}, bf16[64,16,256]{2,1,0:T(8,128)(2,1)}, u32[]{:S(2)}) %copy-start) | copy-done | bytes 524312
  1.7 0.0 copy-start.1
  1.7 0.9 copy-done.1
  2.6 89.8 %shard_map.50 = (bf16[512,1024]{1,0:T(8,128)(2,1)S(1)}, f32[128,16]{1,0:T(8,128)S(1)}) custom-call(s32[64,512]{1,0:T(8,128)S(1)} %bitcast.2, bf16[64,16,256]{2,1,0:T(8,128)(2,1)S(1)} %copy-done, bf16[512,1024]{1,0:T(8,128)(2,1)} %x_hbm.1), custom_call_target="tpu_custom_call" | custom-call | tf_op jit(solution)/shard_map/pallas_call | solution.py:431
  92.4 1.0 %copy.7 = bf16[512,1024]{1,0:T(8,128)(2,1)} copy(bf16[512,1024]{1,0:T(8,128)(2,1)S(1)} %get-tuple-element.8) | data formatting | bytes 2097152
  93.4 0.6 copy.8
Async XLA Ops:
  0.6 1.0 %copy-start = (bf16[64,16,256]{2,1,0:T(8,128)(2,1)S(1)}, bf16[64,16,256]{2,1,0:T(8,128)(2,1)}, u32[]{:S(2)}) copy-start(bf16[64,16,256]{2,1,0:T(8,128)(2,1)} %book_hbm.1) | copy-start | bytes 1572868
  1.7 0.9 copy-start.1

commit v5 on v4

--- a/solution.py
+++ b/solution.py
@@ -464,7 +464,7 @@
         compiler_params=pltpu.CompilerParams(
             collective_id=0, has_side_effects=True, vmem_limit_bytes=52 * 2**20
         ),
-    )(codes.T, codebook, residuals)
+    )(*(pltpu.with_memory_space_constraint(a, pltpu.HBM) for a in (codes.T, codebook, residuals)))
     return rotated, mean.reshape(8, SUBDIM, 16)
 
 

time: 95.1 us -> 94 us (0.988)
  local copies, waits for them, and re-layouts: 3.54 us -> 1.6 us
    unnamed x6 -> x2, local copies, waits for them, and re-layouts: 3.54 us -> 1.6 us
where the time goes in v5:
time: 94 us; the launch traced here: 92.9 us
  Pallas kernels  90.7 us (96%)
  local copies, waits for them, and re-layouts  1.6 us (2%)
    pallas_call x1, Pallas kernels, per_device(): pl.pallas_call(kernel, out_shape=(jax.ShapeDtypeStruct((rows, D), BF16),...  90.7 us

profile of v5, /device:TPU:0, one launch (start us, length us, event | category | flops | bytes accessed | tf_op | source)
XLA Modules:
  0.0 92.9 jit_solution(16486534182243428110)
XLA Ops:
  0.6 90.7 %shard_map.50 = (bf16[512,1024]{1,0:T(8,128)(2,1)S(1)}, f32[128,16]{1,0:T(8,128)S(1)}) custom-call(s32[64,512]{1,0:T(8,128)} %bitcast.3, bf16[64,16,256]{2,1,0:T(8,128)(2,1)} %book_hbm.1, bf16[512,1024]{1,0:T(8,128)(2,1)} %x_hbm.1), custom_call_target="tpu_custom_call" | custom-call | tf_op jit(solution)/shard_map/pallas_call | solution.py:431
  91.3 1.0 %copy.7 = bf16[512,1024]{1,0:T(8,128)(2,1)} copy(bf16[512,1024]{1,0:T(8,128)(2,1)S(1)} %get-tuple-element.8) | data formatting | bytes 2097152
  92.3 0.6 copy.8

commit v6 on v5

--- a/solution.py
+++ b/solution.py
@@ -165,7 +165,6 @@
 
     lax.fori_loop(0, SUBS, rebuild, 0, unroll=8)
     copies[2].wait()
-    here.meet()
 
     mine, theirs = rows_of(core * 512, 512), rows_of((1 - core) * 512, 512)
     flight, base = {}, {}
@@ -229,6 +228,8 @@
     for first in range(0, D, STEP):
         cols = pl.ds(first, STEP)
         part[:, cols] = dot(recon[...], x[:, cols])
+        if first == 0:
+            here.meet()
         for t in range(len(CHUNKS)):
             if first <= CHUNKS[t][0] < first + STEP:
                 stage_core(t)
@@ -360,13 +361,6 @@
     one = jnp.ones((1, 1), F32)
     polynomial(one, one)
 
-    arrive(count_flight)
-    count = (countx[3] + county[0]) + (county[1] + county[2])
-    row = lax.broadcasted_iota(jnp.int32, (LANES, LANES), 0)
-    col = lax.broadcasted_iota(jnp.int32, (LANES, LANES), 1)
-    spread = jnp.where(row == (y * 2 + core) * 8 + col // SUBDIM, 1.0, 0.0)
-    count = jnp.dot(count, spread, precision=lax.Precision.HIGHEST, preferred_element_type=F32)
-
     turned = {}
 
     def turn(pair_of_bands):
@@ -415,6 +409,14 @@
     tally(3)
     spray(2)
     spray(3)
+
+    arrive(count_flight)
+    count = (countx[3] + county[0]) + (county[1] + county[2])
+    row = lax.broadcasted_iota(jnp.int32, (LANES, LANES), 0)
+    col = lax.broadcasted_iota(jnp.int32, (LANES, LANES), 1)
+    spread = jnp.where(row == (y * 2 + core) * 8 + col // SUBDIM, 1.0, 0.0)
+    count = jnp.dot(count, spread, precision=lax.Precision.HIGHEST, preferred_element_type=F32)
+
     sums = jnp.zeros((16, LANES), F32)
     arrive(landed)
     for n in range(64):

time: 94 us -> 93.7 us (level)
  no operation moved by 1% of the time
where the time goes in v6:
time: 93.7 us; the launch traced here: 92.6 us
  Pallas kernels  90.4 us (96%)
  local copies, waits for them, and re-layouts  1.6 us (2%)
    pallas_call x1, Pallas kernels, per_device(): pl.pallas_call(kernel, out_shape=(jax.ShapeDtypeStruct((rows, D), BF16),...  90.4 us

profile of v6, /device:TPU:0, one launch (start us, length us, event | category | flops | bytes accessed | tf_op | source)
XLA Modules:
  0.0 92.6 jit_solution(14002797880390243462)
XLA Ops:
  0.6 90.4 %shard_map.50 = (bf16[512,1024]{1,0:T(8,128)(2,1)S(1)}, f32[128,16]{1,0:T(8,128)S(1)}) custom-call(s32[64,512]{1,0:T(8,128)} %bitcast.3, bf16[64,16,256]{2,1,0:T(8,128)(2,1)} %book_hbm.1, bf16[512,1024]{1,0:T(8,128)(2,1)} %x_hbm.1), custom_call_target="tpu_custom_call" | custom-call | tf_op jit(solution)/shard_map/pallas_call | solution.py:433
  91.0 1.0 %copy.7 = bf16[512,1024]{1,0:T(8,128)(2,1)} copy(bf16[512,1024]{1,0:T(8,128)(2,1)S(1)} %get-tuple-element.8) | data formatting | bytes 2097152
  92.0 0.6 copy.8
